TPU v7x, 32 devices: a whole 2x2x4 slice. The times are simulated.
32 devices in a mesh: req: 8 (over z, y), tp: 4 (over x, core).
Axes of the slice: x: 2, y: 2, z: 4, core: 2. Of those that a mesh axis runs over, the one named last changes fastest.
Arguments:
- tokens: bfloat16 [4096, 2048], P('req')
- token_request_number: int32 [8, 512], P('req'), may hold values from 0 to 7, never falling along the last dimension, each value on 1 to 256 neighbouring positions
- request_adapter_position: int32 [8, 8], P('req'), may hold values from 0 to 15
- adapters_in_use: int32 [16], replicated, may hold values from 0 to 15, as said below
- adapter_storage_slot: int32 [16], replicated, may hold values from 0 to 15, each once
- input_norm_gain: bfloat16 [2048], replicated, may hold values from 0.5 to 1.5
- query_weight: bfloat16 [2048, 2048], P('req', 'tp')
- key_weight: bfloat16 [2048, 2048], P('req', 'tp')
- value_weight: bfloat16 [2048, 2048], P('req', 'tp'), may hold values from -0.125 to 0.125
- output_weight: bfloat16 [2048, 2048], P('tp', 'req'), may hold values from -0.125 to 0.125
- adapter_down_weight: bfloat16 [16, 2, 16, 2048], P('req'), may hold values from -0.125 to 0.125
- adapter_up_weight: bfloat16 [16, 2, 16, 2048], P('req', None, None, 'tp'), may hold values from -0.75 to 0.75
Outputs:
- layer_out: bfloat16 [4096, 2048], P('req', 'tp')
Inputs may be any that keep to these rules, and one draw needn't show every extreme that they name: `adapters_in_use`: 16 different adapter numbers; 0 and 15 are always among them. `token_request_number`: the 512 tokens of each index of req form exactly 8 requests in order, each of 1 to 256 tokens, and one of exactly 256.
All inputs are finite; a program needn't handle non-finite values.
Results may differ from a plain program's by a relative error of at most 0.01.
Values may be sent and summed in bfloat16 or wider, within the bound.
A program may use at most 64 MiB of HBM per device.

v0:
```python
import jax
import jax.numpy as jnp
from jax import lax
from jax.sharding import PartitionSpec as P

HEAD_WIDTH = 64
norm_eps = 1e-05
rope_base = 130000.0
adapter_scale = 2.0


def fetch_adapters(down_part, up_part, active_slots, request_adapters, req_total):
    slot_total = down_part.shape[0]
    stored = jnp.concatenate([down_part, up_part], axis=1)
    split = down_part.shape[1]
    if slot_total * req_total <= 2 * active_slots.shape[0]:
        fetched = lax.all_gather(stored, "req", axis=0, tiled=True)
        places = active_slots[request_adapters]
    else:
        own = active_slots // slot_total == lax.axis_index("req")
        rows = jnp.where(
            own[:, None],
            jnp.take(stored, active_slots % slot_total, axis=0),
            jnp.zeros((), stored.dtype),
        )
        fetched = lax.psum(rows, "req")
        places = request_adapters
    return (fetched[:, :split], fetched[:, split:], places)


def positions_of(segment):
    ordinal = jnp.arange(segment.shape[0], dtype=jnp.int32)
    starts = jnp.concatenate([jnp.ones((1,), jnp.bool_), segment[1:] != segment[:-1]])
    segment_start = lax.cummax(jnp.where(starts, ordinal, jnp.zeros_like(ordinal)), axis=0)
    return ordinal - segment_start


def apply_rotation(values, token_positions):
    half_dim = HEAD_WIDTH // 2
    frequency = rope_base ** (-(jnp.arange(half_dim, dtype=jnp.float32) * 2.0 / HEAD_WIDTH))
    angles = token_positions.astype(jnp.float32)[:, None] * frequency[None, :]
    cosine = jnp.cos(angles)[:, None, :]
    sine_part = jnp.sin(angles)[:, None, :]
    first_half = values[..., :half_dim]
    second_half = values[..., half_dim:]
    return jnp.concatenate(
        [
            first_half * cosine - second_half * sine_part,
            second_half * cosine + first_half * sine_part,
        ],
        axis=-1,
    )


def attend(query_per_head, key_heads, value_per_head, segment):
    scores = (
        jnp.einsum("qhd,khd->hqk", query_per_head, key_heads, preferred_element_type=jnp.float32)
        * 0.125
    )
    ordinal = jnp.arange(segment.shape[0], dtype=jnp.int32)
    allowed = (segment[:, None] == segment[None, :]) & (ordinal[None, :] <= ordinal[:, None])
    scores = jnp.where(allowed[None], scores, jnp.float32(-1e30))
    row_peak = jnp.max(scores, axis=-1, keepdims=True)
    exponent = jnp.where(allowed[None], jnp.exp(scores - row_peak), jnp.float32(0.0))
    weights = (exponent / jnp.sum(exponent, axis=-1, keepdims=True)).astype(jnp.bfloat16)
    return jnp.einsum(
        "hqk,khd->qhd", weights, value_per_head, preferred_element_type=jnp.float32
    ).astype(jnp.bfloat16)


def local(
    tokens,
    token_request_number,
    request_adapter_position,
    adapters_in_use,
    adapter_storage_slot,
    input_norm_gain,
    query_weight,
    key_weight,
    value_weight,
    output_weight,
    adapter_down_weight,
    adapter_up_weight,
):
    row_total, model_width = tokens.shape
    local_width = query_weight.shape[1]
    reduced_rows = adapter_down_weight.shape[2]
    active_count = adapters_in_use.shape[0]
    slot_total = adapter_down_weight.shape[0]
    segment = token_request_number[0]
    request_adapters = request_adapter_position[0]
    tp_total = lax.axis_size("tp")
    req_total = lax.axis_size("req")
    part_rows = reduced_rows // tp_total
    down_part = lax.dynamic_slice_in_dim(
        adapter_down_weight, lax.axis_index("tp") * part_rows, part_rows, 2
    ).reshape(slot_total, 2 * part_rows * model_width)
    up_part = adapter_up_weight.reshape(slot_total, 2 * reduced_rows * local_width)
    down_all, up_all, request_places = fetch_adapters(
        down_part,
        up_part,
        jnp.take(adapter_storage_slot, adapters_in_use, axis=0),
        request_adapters,
        req_total,
    )
    place_total = down_all.shape[0]
    floats = tokens.astype(jnp.float32)
    normed = (
        floats
        * lax.rsqrt(jnp.mean(floats * floats, axis=-1, keepdims=True) + norm_eps)
        * input_norm_gain.astype(jnp.float32)
    ).astype(jnp.bfloat16)
    query_plain = jnp.dot(
        normed,
        lax.all_gather(query_weight, "req", axis=0, tiled=True),
        preferred_element_type=jnp.float32,
    )
    key_base = jnp.dot(
        normed,
        lax.all_gather(key_weight, "req", axis=0, tiled=True),
        preferred_element_type=jnp.float32,
    )
    value_plain = jnp.dot(
        normed,
        lax.all_gather(value_weight, "req", axis=0, tiled=True),
        preferred_element_type=jnp.float32,
    )
    request_total = request_adapters.shape[0]
    member = segment[:, None] == jnp.arange(request_total, dtype=jnp.int32)[None, :]
    token_place = jnp.sum(
        jnp.where(member, request_places[None, :], jnp.zeros_like(request_places)[None, :]), axis=1
    )
    share = 2 * part_rows
    shrunk_all = lax.dot_general(
        normed,
        down_all.reshape(place_total * share, model_width),
        (((1,), (1,)), ((), ())),
        preferred_element_type=jnp.float32,
    ).astype(jnp.bfloat16)
    column = jnp.arange(place_total * share, dtype=jnp.int32)
    kept = jnp.where(
        token_place[:, None] == (column // share)[None, :], shrunk_all, jnp.zeros((), jnp.bfloat16)
    )
    fold = (column % share)[:, None] == jnp.arange(share, dtype=jnp.int32)[None, :]
    shrunk_part = jnp.dot(
        kept, fold.astype(jnp.bfloat16), preferred_element_type=jnp.float32
    ).astype(jnp.bfloat16)
    shrunk = lax.all_gather(shrunk_part, "tp", axis=1, tiled=True)
    source = jnp.arange(tp_total * share, dtype=jnp.int32)
    source_kind = source % share // part_rows
    source_rank = source // share * part_rows + source % part_rows
    target = jnp.arange(place_total * reduced_rows, dtype=jnp.int32)
    mine = token_place[:, None] == (target // reduced_rows)[None, :]
    up_all = up_all.reshape(place_total, 2, reduced_rows, local_width)

    def change_of(kind):
        spread_map = (source_kind == kind)[:, None] & (
            source_rank[:, None] == (target % reduced_rows)[None, :]
        )
        spread = jnp.dot(
            shrunk, spread_map.astype(jnp.bfloat16), preferred_element_type=jnp.float32
        ).astype(jnp.bfloat16)
        spread = jnp.where(mine, spread, jnp.zeros((), jnp.bfloat16))
        return jnp.dot(
            spread,
            up_all[:, kind].reshape(place_total * reduced_rows, local_width),
            preferred_element_type=jnp.float32,
        )

    query_change = change_of(0)
    value_change = change_of(1)
    head_total = local_width // HEAD_WIDTH
    token_positions = positions_of(segment)
    query_per_head = apply_rotation(
        (query_plain + adapter_scale * query_change).reshape(row_total, head_total, HEAD_WIDTH),
        token_positions,
    ).astype(jnp.bfloat16)
    key_heads = apply_rotation(
        key_base.reshape(row_total, head_total, HEAD_WIDTH), token_positions
    ).astype(jnp.bfloat16)
    value_per_head = (
        (value_plain + adapter_scale * value_change)
        .astype(jnp.bfloat16)
        .reshape(row_total, head_total, HEAD_WIDTH)
    )
    attended = attend(query_per_head, key_heads, value_per_head, segment).reshape(
        row_total, local_width
    )
    partial_out = jnp.dot(
        attended,
        lax.all_gather(output_weight, "req", axis=1, tiled=True),
        preferred_element_type=jnp.float32,
    )
    summed = lax.psum_scatter(
        partial_out.astype(jnp.bfloat16), "tp", scatter_dimension=1, tiled=True
    ).astype(jnp.float32)
    share_width = summed.shape[1]
    residual_part = lax.dynamic_slice_in_dim(
        tokens, lax.axis_index("tp") * share_width, share_width, 1
    )
    return (summed + residual_part.astype(jnp.float32)).astype(jnp.bfloat16)


def solution(mesh):
    in_specs = (
        P("req", None),
        P("req", None),
        P("req", None),
        P(),
        P(),
        P(),
        P("req", "tp"),
        P("req", "tp"),
        P("req", "tp"),
        P("tp", "req"),
        P("req", None, None, None),
        P("req", None, None, "tp"),
    )
    out_specs = P("req", "tp")
    return jax.shard_map(local, mesh=mesh, in_specs=in_specs, out_specs=out_specs, check_vma=False)
```

profile of v0, /device:TPU:0, one launch (start us, length us, event | category | flops | bytes accessed | tf_op | source)
XLA Modules:
  0.0 296.7 jit_solution(14154784594400048160)
XLA Ops:
  6.5 0.0 copy-start
  6.5 0.0 copy-start.6
  6.5 0.0 copy-start.1
  6.5 0.0 all-gather.15.cloned.1.call-start
  6.6 1.0 copy.18
  7.6 0.0 copy-done
  7.7 0.1 reshape.292
  7.7 0.8 maximum_bitcast_fusion
  8.5 0.0 all-gather.15.cloned.1.call-update
  8.5 0.0 all-gather.7.cloned.1.call-start
  8.6 0.7 all-gather.7.cloned.1.call-update
  9.3 0.0 all-gather.9.cloned.1.call-start
  9.3 0.7 all-gather.9.cloned.1.call-update
  10.0 0.0 all-gather.11.cloned.1.call-start
  10.1 0.5 all-gather.11.cloned.1.call-update
  10.6 0.0 all-gather.13.cloned.1.call-start
  10.6 0.5 all-gather.13.cloned.1.call-update
  11.2 0.0 reduce-scatter.2.cloned.1.call-start
  11.3 0.7 convert_element_type.59
  12.0 2.1 fusion.2
  14.1 0.7 compare_select_fusion.1
  14.8 0.0 copy-done.1
  14.8 0.7 gather_fusion
  15.4 0.0 copy-done.6
  15.4 0.0 copy-start.2
  15.5 0.0 copy-done.7
  15.5 0.0 copy-done.5
  15.5 0.1 compare_reduce_fusion
  15.6 0.9 fusion.18
  16.5 0.6 gather_fusion.1
  17.1 0.1 select_reduce_fusion
  17.2 0.1 add_select_fusion
  17.3 0.3 reduce-window.9
  17.6 0.1 slice.46
  17.7 0.1 slice_reduce_fusion
  17.8 0.1 fusion.47
  17.9 0.9 multiply_cosine_fusion
  18.9 33.5 %all-gather.15.cloned.1.call-done = bf16[8,2,32768]{2,1,0:T(2,128)(2,1)} async-done(((bf16[1,2,32768]{2,1,0:T(2,128)(2,1)}), bf16[8,2,32768]{2,1,0:T(2,128)(2,1)}) %all-gather.15.cloned.1.call-update) | async-done | bytes 1048592 | tf_op jit(solution)/shard_map/all_gather | solution.py:17
  52.4 1.5 reshape.319
  53.9 0.9 fusion.70
  54.7 0.2 copy.19
  54.9 0.9 fusion.71
  55.8 1.3 reshape.294
  57.0 0.0 copy-done.2
  57.0 0.9 fusion.17
  58.0 5.4 %all_gather.20 = bf16[512,32]{0,1:T(8,128)(2,1)S(1)} all-gather(bf16[512,8]{0,1:T(8,128)(2,1)S(1)} %fusion.17), channel_id=1, replica_groups=mesh['req'=8,'tp'=4] {'tp'}, dimensions={1}, use_global_device_ids=true | all-gather | bytes 40960 | tf_op jit(solution)/shard_map/all_gather | solution.py:148
  63.4 39.2 %all-gather.7.cloned.1.call-done = bf16[2048,512]{1,0:T(8,128)(2,1)} async-done(((bf16[256,512]{1,0:T(8,128)(2,1)}), bf16[2048,512]{1,0:T(8,128)(2,1)}) %all-gather.7.cloned.1.call-update) | async-done | bytes 2097168 | tf_op jit(solution)/shard_map/all_gather | solution.py:125
  102.6 3.0 %fusion.68 = f32[512,512]{0,1:T(8,128)S(1)} fusion(bf16[2048,512]{1,0:T(8,128)(2,1)} %all-gather.7.cloned.1.call-done, bf16[512,2048]{1,0:T(8,128)(2,1)S(1)} %copy-done.2, f32[2048]{0:T(1024)S(1)} %convert_element_type.59, f32[512]{0:T(512)S(1)} %add_rsqrt_fusion), kind=kOutput, calls=%fused_computation.120 | convolution fusion | flops 1077936128 | bytes 5253120 | tf_op jit(solution)/shard_map/dot_general | solution.py:123
  105.6 2.3 fusion.12
  107.9 44.7 %all-gather.9.cloned.1.call-done = bf16[2048,512]{1,0:T(8,128)(2,1)} async-done(((bf16[256,512]{1,0:T(8,128)(2,1)}), bf16[2048,512]{1,0:T(8,128)(2,1)}) %all-gather.9.cloned.1.call-update) | async-done | bytes 2097168 | tf_op jit(solution)/shard_map/all_gather | solution.py:115
  152.5 3.9 %fusion.64 = f32[512,512]{0,1:T(8,128)} fusion(bf16[2048,512]{1,0:T(8,128)(2,1)} %all-gather.9.cloned.1.call-done, bf16[512,2048]{1,0:T(8,128)(2,1)S(1)} %copy-done.2, f32[2048]{0:T(1024)S(1)} %convert_element_type.59, f32[512]{0:T(512)S(1)} %add_rsqrt_fusion), kind=kOutput, calls=%fused_computation.119 | convolution fusion | flops 1077936128 | bytes 5253120 | tf_op jit(solution)/shard_map/dot_general | solution.py:113
  156.5 1.9 fusion.9
  158.4 44.0 %all-gather.11.cloned.1.call-done = bf16[2048,512]{1,0:T(8,128)(2,1)} async-done(((bf16[256,512]{1,0:T(8,128)(2,1)}), bf16[2048,512]{1,0:T(8,128)(2,1)}) %all-gather.11.cloned.1.call-update) | async-done | bytes 2097168 | tf_op jit(solution)/shard_map/all_gather | solution.py:120
  202.3 3.0 %fusion.62 = f32[512,512]{0,1:T(8,128)S(1)} fusion(bf16[2048,512]{1,0:T(8,128)(2,1)} %all-gather.11.cloned.1.call-done, bf16[512,2048]{1,0:T(8,128)(2,1)S(1)} %copy-done.2, f32[2048]{0:T(1024)S(1)} %convert_element_type.59, f32[512]{0:T(512)S(1)} %add_rsqrt_fusion), kind=kOutput, calls=%fused_computation.118 | convolution fusion | flops 1077936128 | bytes 5253120 | tf_op jit(solution)/shard_map/dot_general | solution.py:118
  205.3 0.0 copy-done.4
  205.4 1.3 subtract_convert_fusion.1
  206.7 8.2 %fusion.72 = (f32[8,512]{1,0:T(8,128)S(1)}, f32[8,512,512]{1,2,0:T(8,128)}) fusion(pred[512,512]{0,1:T(8,128)(4,1)} %fusion.18, bf16[512,8,32]{0,2,1:T(8,128)(2,1)} %get-tuple-element.13, bf16[512,8,32]{0,2,1:T(8,128)(2,1)} %get-tuple-element.14, bf16[512,8,32]{0,2,1:T(8,128)(2,1)} %get-tuple-element.6, bf16[512,8,32]{0,2,1:T(8,128)(2,1)} %get-tuple-element.5), kind=kOutput, calls=%fused_computation.123 | convolution fusion | flops 281018880 | bytes 9715712 | tf_op jit(solution)/shard_map/sub | solution.py:64
  214.9 0.0 copy-done.3
  214.9 4.3 %fusion.11 = bf16[8,64,512]{2,1,0:T(8,128)(2,1)S(1)} fusion(bf16[512,8,64]{0,2,1:T(8,128)(2,1)S(1)} %bitcast.46, f32[8,512,512]{1,2,0:T(8,128)} %get-tuple-element.18, f32[8,512]{1,0:T(8,128)S(1)} %get-tuple-element.17), kind=kOutput, calls=%fused_computation.21 | convolution fusion | flops 272891904 | bytes 9453568 | tf_op jit(solution)/shard_map/hqk,khd->qhd/dot_general | solution.py:66
  219.2 34.7 %all-gather.13.cloned.1.call-done = bf16[512,2048]{1,0:T(8,128)(2,1)} async-done(((bf16[512,256]{1,0:T(8,128)(2,1)}), bf16[512,2048]{1,0:T(8,128)(2,1)}) %all-gather.13.cloned.1.call-update) | async-done | bytes 2097168 | tf_op jit(solution)/shard_map/all_gather | solution.py:191
  253.8 4.2 %convolution_convert_fusion = bf16[512,2048]{1,0:T(8,128)(2,1)} fusion(bf16[512,512]{0,1:T(8,128)(2,1)S(1)} %bitcast.51, bf16[512,2048]{1,0:T(8,128)(2,1)} %all-gather.13.cloned.1.call-done), kind=kOutput, calls=%fused_computation.16 | convolution fusion | flops 1074790400 | bytes 4718592 | tf_op jit(solution)/shard_map/dot_general | solution.py:189
  258.0 0.0 reduce-scatter.2.cloned.1.call-update
  258.1 29.8 %reduce-scatter.2.cloned.1.call-done = bf16[512,512]{1,0:T(8,128)(2,1)} async-done(((bf16[512,2048]{1,0:T(8,128)(2,1)}), bf16[512,512]{1,0:T(8,128)(2,1)}) %reduce-scatter.2.cloned.1.call-update) | async-done | bytes 524304 | tf_op jit(solution)/shard_map/reduce_scatter | solution.py:194
  287.8 2.0 add_convert_fusion
  (17 shorter events, 0.2 us)
Async XLA Ops:
  6.5 1.1 copy-start
  6.5 8.9 %copy-start.6 = (s32[16]{0:T(128)S(1)}, s32[16]{0:T(128)}, u32[]{:S(2)}) copy-start(s32[16]{0:T(128)} %param.15) | copy-start | bytes 196
  6.5 8.2 %copy-start.1 = (s32[16]{0:T(128)S(1)}, s32[16]{0:T(128)}, u32[]{:S(2)}) copy-start(s32[16]{0:T(128)} %param.16) | copy-start | bytes 196
  6.5 8.9 %copy-start.7 = (s32[1,8]{1,0:T(1,128)S(1)}, s32[1,8]{1,0:T(1,128)}, u32[]{:S(2)}) copy-start(s32[1,8]{1,0:T(1,128)} %param.14) | copy-start | bytes 100
  6.5 8.9 %copy-start.5 = (s32[1,512]{1,0:T(1,128)S(1)}, s32[1,512]{1,0:T(1,128)}, u32[]{:S(2)}) copy-start(s32[1,512]{1,0:T(1,128)} %param.13) | copy-start | bytes 6148
  6.5 45.8 %all-gather.15.cloned.1.call-start = ((), (), s32[]{:S(2)}) async-start(), calls=%async_computation.6 | async-start | bytes 1179648 | tf_op jit(solution)/shard_map/all_gather | solution.py:17
  8.5 94.1 %all-gather.7.cloned.1.call-start = ((), (), s32[]{:S(2)}) async-start(), calls=%async_computation.1 | async-start | bytes 2359296 | tf_op jit(solution)/shard_map/all_gather | solution.py:125
  9.3 143.3 %all-gather.9.cloned.1.call-start = ((), (), s32[]{:S(2)}) async-start(), calls=%async_computation.2 | async-start | bytes 2359296 | tf_op jit(solution)/shard_map/all_gather | solution.py:115
  10.0 192.3 %all-gather.11.cloned.1.call-start = ((), (), s32[]{:S(2)}) async-start(), calls=%async_computation.3 | async-start | bytes 2359296 | tf_op jit(solution)/shard_map/all_gather | solution.py:120
  10.6 243.2 %all-gather.13.cloned.1.call-start = ((), (), s32[]{:S(2)}) async-start(), calls=%async_computation.4 | async-start | bytes 2359296 | tf_op jit(solution)/shard_map/all_gather | solution.py:191
  11.2 276.6 %reduce-scatter.2.cloned.1.call-start = ((), (), s32[]{:S(2)}) async-start(), calls=%async_computation.5 | async-start | bytes 2621440 | tf_op jit(solution)/shard_map/reduce_scatter | solution.py:194
  15.4 41.6 %copy-start.2 = (bf16[512,2048]{1,0:T(8,128)(2,1)S(1)}, bf16[512,2048]{1,0:T(8,128)(2,1)}, u32[]{:S(2)}) copy-start(bf16[512,2048]{1,0:T(8,128)(2,1)} %param.12) | copy-start | bytes 6291460
  202.3 3.0 %copy-start.4 = (f32[512,32]{0,1:T(8,128)S(1)}, f32[512,32]{0,1:T(8,128)}, u32[]{:S(2)}) copy-start(f32[512,32]{0,1:T(8,128)} %get-tuple-element.16) | copy-start | bytes 196612
  206.7 8.2 %copy-start.3 = (bf16[512,512]{0,1:T(8,128)(2,1)S(1)}, bf16[512,512]{0,1:T(8,128)(2,1)}, u32[]{:S(2)}) copy-start(bf16[512,512]{0,1:T(8,128)(2,1)} %fusion.12) | copy-start | bytes 1572868
Sparse Core Ops, SparseCore 0:
  9.5 42.8 all-gather.14
  54.5 48.0 all-gather.6
  104.7 47.7 all-gather.8
  154.5 47.7 all-gather.10
  204.2 49.5 all-gather.12
  258.2 29.5 reduce-scatter.1
where the time goes:
time: 297 us
  waiting for transfers between devices  228 us (77%)
  matrix products  31.7 us (11%)
  between operations  13.7 us (5%)
  other arithmetic  10.1 us (3%)
  local copies, waits for them, and re-layouts  7.27 us (2%)
  blocking collectives  5.39 us (2%)
    all_gather x1, waiting for transfers between devices, local(): lax.all_gather(query_weight, 'req', axis=0, tiled=True)  44.7 us
    all_gather x1, waiting for transfers between devices, local(): lax.all_gather(key_weight, 'req', axis=0, tiled=True)  44 us
    all_gather x1, waiting for transfers between devices, local(): lax.all_gather(value_weight, 'req', axis=0, tiled=True)  39.2 us
    all_gather x1, waiting for transfers between devices, local(): lax.all_gather(output_weight, 'req', axis=1, tiled=True)  34.7 us
    all_gather x1, waiting for transfers between devices, fetch_adapters(): fetched = lax.all_gather(stored, 'req', axis=0, tiled=True)  33.5 us
    reduce_scatter x1, waiting for transfers between devices, local(): lax.psum_scatter(partial_out.astype(jnp.bfloat16), 'tp', scatter_dimensio...  29.8 us
    sub x1, matrix products, attend(): scores - row_peak  8.2 us
  transfers between devices with their start and end apart: 6, of which 6 were waited for; matrix products, arithmetic and copies ran while one was open for 14% of the time, Pallas kernels for 0%

commit v1 on v0

--- a/solution.py
+++ b/solution.py
@@ -7,6 +7,27 @@
 norm_eps = 1e-05
 rope_base = 130000.0
 adapter_scale = 2.0
+
+
+def start_sheets_for(x0, on_dim):
+    side_arr = list(x0.shape[1:])
+    side_arr[on_dim] *= x0.shape[0]
+    lower = jnp.moveaxis(x0, 0, on_dim).reshape(side_arr)
+    return lower
+
+
+def guide_meshes_all(slab_in, chip_axis):
+    new = slab_in[None]
+    n_dev_all = lax.axis_size(chip_axis)
+    for h in range(n_dev_all.bit_length() - 1):
+        f_now = 1 << h
+        current_block = lax.ppermute(
+            new, axis_name=chip_axis, perm=list(map(lambda kk: (kk, kk ^ f_now), range(n_dev_all)))
+        )
+        vec_out = jnp.stack([new, current_block])
+        big = lax.axis_index(chip_axis) >> h & 1
+        new = jnp.where(big == 0, vec_out, vec_out[::-1]).reshape(-1, *slab_in.shape)
+    return new
 
 
 def fetch_adapters(down_part, up_part, active_slots, request_adapters, req_total):
@@ -82,6 +103,11 @@
     adapter_down_weight,
     adapter_up_weight,
 ):
+
+    def cubes_convert(u, payload, along_dim):
+        high = start_sheets_for(guide_meshes_all(payload, u), along_dim)
+        return high
+
     row_total, model_width = tokens.shape
     local_width = query_weight.shape[1]
     reduced_rows = adapter_down_weight.shape[2]
@@ -111,9 +137,7 @@
         * input_norm_gain.astype(jnp.float32)
     ).astype(jnp.bfloat16)
     query_plain = jnp.dot(
-        normed,
-        lax.all_gather(query_weight, "req", axis=0, tiled=True),
-        preferred_element_type=jnp.float32,
+        normed, cubes_convert("req", query_weight, 0), preferred_element_type=jnp.float32
     )
     key_base = jnp.dot(
         normed,

time: 297 us -> 275 us (0.926)
  waiting for transfers between devices: 228 us -> 193 us
  starting transfers between devices: 0.23 us -> 7.6 us
    all_gather x1 -> x0, waiting for transfers between devices: 44.7 us -> none  [local(): lax.all_gather(query_weight, 'req', axis=0, tiled=True)]
    ppermute x0 -> x3, waiting for transfers between devices: none -> 23.3 us  [guide_meshes_all(): lax.ppermute(new, axis_name=chip_axis, perm=list(map(lambda kk: (kk, kk ^...]
    all_gather x1, waiting for transfers between devices: 39.2 us -> 23.4 us  [local(): lax.all_gather(value_weight, 'req', axis=0, tiled=True)]
    ppermute x0 -> x3, starting transfers between devices: none -> 7.45 us  [guide_meshes_all(): lax.ppermute(new, axis_name=chip_axis, perm=list(map(lambda kk: (kk, kk ^...]
    all_gather x1, waiting for transfers between devices: 33.5 us -> 37.1 us  [fetch_adapters(): fetched = lax.all_gather(stored, 'req', axis=0, tiled=True)]
  transfers between devices with their start and end apart: 6 -> 8, of which waited for: 6 -> 8; matrix products, arithmetic and copies ran while one was open for 14% -> 17% of each run, Pallas kernels for 0% -> 0%
where the time goes in v1:
time: 275 us
  waiting for transfers between devices  193 us (70%)
  matrix products  33 us (12%)
  between operations  13.4 us (5%)
  other arithmetic  12.4 us (5%)
  local copies, waits for them, and re-layouts  9.82 us (4%)
  starting transfers between devices  7.6 us (3%)
  blocking collectives  5.39 us (2%)
    all_gather x1, waiting for transfers between devices, local(): lax.all_gather(key_weight, 'req', axis=0, tiled=True)  43.3 us
    all_gather x1, waiting for transfers between devices, fetch_adapters(): fetched = lax.all_gather(stored, 'req', axis=0, tiled=True)  37.1 us
    all_gather x1, waiting for transfers between devices, local(): lax.all_gather(output_weight, 'req', axis=1, tiled=True)  34.7 us
    reduce_scatter x1, waiting for transfers between devices, local(): lax.psum_scatter(partial_out.astype(jnp.bfloat16), 'tp', scatter_dimensio...  29.8 us
    all_gather x1, waiting for transfers between devices, local(): lax.all_gather(value_weight, 'req', axis=0, tiled=True)  23.4 us
    ppermute x3, waiting for transfers between devices, guide_meshes_all(): lax.ppermute(new, axis_name=chip_axis, perm=list(map(lambda kk: (kk, kk ^...  23.3 us
    sub x1, matrix products, attend(): scores - row_peak  8.19 us
    ppermute x3, starting transfers between devices, guide_meshes_all(): lax.ppermute(new, axis_name=chip_axis, perm=list(map(lambda kk: (kk, kk ^...  7.45 us
  transfers between devices with their start and end apart: 8, of which 8 were waited for; matrix products, arithmetic and copies ran while one was open for 17% of the time, Pallas kernels for 0%

profile of v1, /device:TPU:0, one launch (start us, length us, event | category | flops | bytes accessed | tf_op | source)
XLA Modules:
  0.0 274.7 jit_solution(8003591898480120133)
XLA Ops:
  6.6 0.0 copy-start.10
  6.6 0.0 copy-start.7
  6.6 0.9 copy.18
  7.6 0.1 reshape.298
  7.7 0.8 maximum_bitcast_fusion
  8.4 0.0 all-gather.12.cloned.1.call-update
  8.5 0.0 all-gather.6.cloned.1.call-start
  8.5 0.7 all-gather.6.cloned.1.call-update
  9.2 0.0 all-gather.8.cloned.1.call-start
  9.3 0.7 all-gather.8.cloned.1.call-update
  10.0 0.0 all-gather.10.cloned.1.call-start
  10.0 3.0 %collective-permute-start = (bf16[1,256,512]{2,1,0:T(8,128)(2,1)}, bf16[1,256,512]{2,1,0:T(8,128)(2,1)S(1)}, u32[]{:S(2)}, u32[]{:S(2)}) collective-permute-start(bf16[1,256,512]{2,1,0:T(8,128)(2,1)} %bitcast.64), channel_id=1, source_target_pairs={{0,4},{4,0},{8,12},{12,8},{16,20},{20,16},{24,28},{28,24},{1,5},{5... | collective-permute-start | bytes 786440 | tf_op jit(solution)/shard_map/ppermute | solution.py:24
  13.0 0.0 all-gather.10.cloned.1.call-update
  13.1 0.0 reduce-scatter.2.cloned.1.call-start
  13.2 2.1 fusion.2
  15.3 0.7 gather_fusion
  16.0 0.1 compare_reduce_fusion
  16.1 0.1 add_select_fusion
  16.2 0.3 reduce-window.9
  16.5 0.1 slice.46
  16.6 0.1 slice_reduce_fusion
  16.7 0.6 gather_fusion.1
  17.4 0.1 select_reduce_fusion
  17.5 0.1 fusion.48
  17.6 2.0 collective-permute-done
  19.6 0.1 pad_maximum_fusion.2
  19.6 0.1 fusion.23
  19.7 1.9 collective-permute-start.1
  21.6 0.9 multiply_cosine_fusion
  22.6 0.9 fusion.17
  23.5 13.7 %collective-permute-done.1 = bf16[2,256,512]{2,1,0:T(8,128)(2,1)S(1)} collective-permute-done((bf16[2,256,512]{2,1,0:T(8,128)(2,1)S(1)}, bf16[2,256,512]{2,1,0:T(8,128)(2,1)S(1)}, u32[]{:S(2)}, u32[]{:S(2)}) %collective-permute-start.1) | collective-permute-done | bytes 524320 | tf_op jit(solution)/shard_map/ppermute | solution.py:24
  37.1 0.1 pad_maximum_fusion.1
  37.2 0.2 reverse_select_fusion.1
  37.4 2.6 collective-permute-start.2
  40.0 37.1 %all-gather.12.cloned.1.call-done = bf16[8,2,32768]{2,1,0:T(2,128)(2,1)} async-done(((bf16[1,2,32768]{2,1,0:T(2,128)(2,1)}), bf16[8,2,32768]{2,1,0:T(2,128)(2,1)}) %all-gather.12.cloned.1.call-update) | async-done | bytes 1048592 | tf_op jit(solution)/shard_map/all_gather | solution.py:38
  77.1 1.5 reshape.327
  78.5 0.9 fusion.70
  79.4 1.0 copy.19
  80.4 2.1 reshape.300
  82.5 0.0 copy-done.2
  82.5 2.0 fusion.16
  84.4 5.4 %all_gather.17 = bf16[512,32]{0,1:T(8,128)(2,1)S(1)} all-gather(bf16[512,8]{0,1:T(8,128)(2,1)S(1)} %fusion.16), channel_id=1, replica_groups=mesh['req'=8,'tp'=4] {'tp'}, dimensions={1}, use_global_device_ids=true | all-gather | bytes 40960 | tf_op jit(solution)/shard_map/all_gather | solution.py:172
  89.8 1.8 fusion.71
  91.7 7.6 %collective-permute-done.2 = bf16[4,256,512]{2,1,0:T(8,128)(2,1)} collective-permute-done((bf16[4,256,512]{2,1,0:T(8,128)(2,1)S(1)}, bf16[4,256,512]{2,1,0:T(8,128)(2,1)}, u32[]{:S(2)}, u32[]{:S(2)}) %collective-permute-start.2) | collective-permute-done | bytes 1048608 | tf_op jit(solution)/shard_map/ppermute | solution.py:24
  99.3 1.4 pad_maximum_fusion
  100.7 0.0 copy-start.3
  100.7 1.8 reverse_select_fusion
  102.5 1.6 convolution_multiply_fusion
  104.0 3.2 %convolution_add_fusion = f32[512,512]{0,1:T(8,128)S(1)} fusion(f32[512,512]{0,1:T(8,128)} %convolution_multiply_fusion, bf16[2048,512]{1,0:T(8,128)(2,1)} %bitcast.54, bf16[512,2048]{1,0:T(8,128)(2,1)S(1)} %copy-done.2, f32[2048]{0:T(1024)S(1)} %convert_element_type.59, f32[512]{0:T(512)S(1)} %add_rsqrt_fusion), kind=kOutput, calls=%fused_computation.23 | convolution fusion | flops 1078198272 | bytes 6301696 | tf_op jit(solution)/shard_map/dot_general | solution.py:139
  107.3 23.4 %all-gather.6.cloned.1.call-done = bf16[2048,512]{1,0:T(8,128)(2,1)} async-done(((bf16[256,512]{1,0:T(8,128)(2,1)}), bf16[2048,512]{1,0:T(8,128)(2,1)}) %all-gather.6.cloned.1.call-update) | async-done | bytes 2097168 | tf_op jit(solution)/shard_map/all_gather | solution.py:149
  130.7 3.9 %fusion.68 = f32[512,512]{0,1:T(8,128)} fusion(bf16[2048,512]{1,0:T(8,128)(2,1)} %all-gather.6.cloned.1.call-done, bf16[512,2048]{1,0:T(8,128)(2,1)S(1)} %copy-done.2, f32[2048]{0:T(1024)S(1)} %convert_element_type.59, f32[512]{0:T(512)S(1)} %add_rsqrt_fusion), kind=kOutput, calls=%fused_computation.127 | convolution fusion | flops 1077936128 | bytes 5253120 | tf_op jit(solution)/shard_map/dot_general | solution.py:147
  134.7 2.7 fusion.11
  137.4 43.3 %all-gather.8.cloned.1.call-done = bf16[2048,512]{1,0:T(8,128)(2,1)} async-done(((bf16[256,512]{1,0:T(8,128)(2,1)}), bf16[2048,512]{1,0:T(8,128)(2,1)}) %all-gather.8.cloned.1.call-update) | async-done | bytes 2097168 | tf_op jit(solution)/shard_map/all_gather | solution.py:144
  180.7 3.0 %fusion.63 = f32[512,512]{0,1:T(8,128)S(1)} fusion(bf16[2048,512]{1,0:T(8,128)(2,1)} %all-gather.8.cloned.1.call-done, bf16[512,2048]{1,0:T(8,128)(2,1)S(1)} %copy-done.2, f32[2048]{0:T(1024)S(1)} %convert_element_type.59, f32[512]{0:T(512)S(1)} %add_rsqrt_fusion), kind=kOutput, calls=%fused_computation.126 | convolution fusion | flops 1077936128 | bytes 5253120 | tf_op jit(solution)/shard_map/dot_general | solution.py:142
  183.7 0.0 copy-done.5
  183.7 1.3 subtract_convert_fusion.1
  185.0 8.2 %fusion.72 = (f32[8,512]{1,0:T(8,128)S(1)}, f32[8,512,512]{1,2,0:T(8,128)}) fusion(pred[512,512]{0,1:T(8,128)(4,1)} %fusion.17, bf16[512,8,32]{0,2,1:T(8,128)(2,1)} %get-tuple-element.15, bf16[512,8,32]{0,2,1:T(8,128)(2,1)} %get-tuple-element.16, bf16[512,8,32]{0,2,1:T(8,128)(2,1)} %get-tuple-element.6, bf16[512,8,32]{0,2,1:T(8,128)(2,1)} %get-tuple-element.5), kind=kOutput, calls=%fused_computation.130 | convolution fusion | flops 281018880 | bytes 9715712 | tf_op jit(solution)/shard_map/sub | solution.py:85
  193.2 0.0 copy-done.4
  193.2 4.2 %fusion.10 = bf16[8,64,512]{2,1,0:T(8,128)(2,1)S(1)} fusion(bf16[512,8,64]{0,2,1:T(8,128)(2,1)S(1)} %bitcast.61, f32[8,512,512]{1,2,0:T(8,128)} %get-tuple-element.20, f32[8,512]{1,0:T(8,128)S(1)} %get-tuple-element.19), kind=kOutput, calls=%fused_computation.24 | convolution fusion | flops 272891904 | bytes 9453568 | tf_op jit(solution)/shard_map/hqk,khd->qhd/dot_general | solution.py:87
  197.5 34.7 %all-gather.10.cloned.1.call-done = bf16[512,2048]{1,0:T(8,128)(2,1)} async-done(((bf16[512,256]{1,0:T(8,128)(2,1)}), bf16[512,2048]{1,0:T(8,128)(2,1)}) %all-gather.10.cloned.1.call-update) | async-done | bytes 2097168 | tf_op jit(solution)/shard_map/all_gather | solution.py:215
  232.2 4.2 %convolution_convert_fusion = bf16[512,2048]{1,0:T(8,128)(2,1)} fusion(bf16[512,512]{0,1:T(8,128)(2,1)S(1)} %bitcast.70, bf16[512,2048]{1,0:T(8,128)(2,1)} %all-gather.10.cloned.1.call-done), kind=kOutput, calls=%fused_computation.17 | convolution fusion | flops 1074790400 | bytes 4718592 | tf_op jit(solution)/shard_map/dot_general | solution.py:213
  236.4 0.0 reduce-scatter.2.cloned.1.call-update
  236.4 29.8 %reduce-scatter.2.cloned.1.call-done = bf16[512,512]{1,0:T(8,128)(2,1)} async-done(((bf16[512,2048]{1,0:T(8,128)(2,1)}), bf16[512,512]{1,0:T(8,128)(2,1)}) %reduce-scatter.2.cloned.1.call-update) | async-done | bytes 524304 | tf_op jit(solution)/shard_map/reduce_scatter | solution.py:218
  266.2 2.0 add_convert_fusion
  (32 shorter events, 0.2 us)
Async XLA Ops:
  6.5 1.0 copy-start
  6.5 8.7 %copy-start.9 = (s32[16]{0:T(128)S(1)}, s32[16]{0:T(128)}, u32[]{:S(2)}) copy-start(s32[16]{0:T(128)} %param.15) | copy-start | bytes 196
  6.5 8.7 %copy-start.1 = (s32[16]{0:T(128)S(1)}, s32[16]{0:T(128)}, u32[]{:S(2)}) copy-start(s32[16]{0:T(128)} %param.16) | copy-start | bytes 196
  6.5 70.5 %all-gather.12.cloned.1.call-start = ((), (), s32[]{:S(2)}) async-start(), calls=%async_computation.5 | async-start | bytes 1179648 | tf_op jit(solution)/shard_map/all_gather | solution.py:38
  6.6 9.4 %copy-start.10 = (s32[1,8]{1,0:T(1,128)S(1)}, s32[1,8]{1,0:T(1,128)}, u32[]{:S(2)}) copy-start(s32[1,8]{1,0:T(1,128)} %param.14) | copy-start | bytes 100
  6.6 9.4 %copy-start.7 = (s32[1,512]{1,0:T(1,128)S(1)}, s32[1,512]{1,0:T(1,128)}, u32[]{:S(2)}) copy-start(s32[1,512]{1,0:T(1,128)} %param.13) | copy-start | bytes 6148
  8.4 9.0 %copy-start.8 = (bf16[2048]{0:T(1024)(128)(2,1)S(1)}, bf16[2048]{0:T(1024)(128)(2,1)}, u32[]{:S(2)}) copy-start(bf16[2048]{0:T(1024)(128)(2,1)} %param.17) | copy-start | bytes 12292
  8.4 11.1 %copy-start.6 = (bf16[256,512]{1,0:T(8,128)(2,1)S(1)}, bf16[256,512]{1,0:T(8,128)(2,1)}, u32[]{:S(2)}) copy-start(bf16[256,512]{1,0:T(8,128)(2,1)} %param.18) | copy-start | bytes 786436
  8.5 122.3 %all-gather.6.cloned.1.call-start = ((), (), s32[]{:S(2)}) async-start(), calls=%async_computation.1 | async-start | bytes 2359296 | tf_op jit(solution)/shard_map/all_gather | solution.py:149
  9.2 171.5 %all-gather.8.cloned.1.call-start = ((), (), s32[]{:S(2)}) async-start(), calls=%async_computation.2 | async-start | bytes 2359296 | tf_op jit(solution)/shard_map/all_gather | solution.py:144
  10.0 222.2 %all-gather.10.cloned.1.call-start = ((), (), s32[]{:S(2)}) async-start(), calls=%async_computation.3 | async-start | bytes 2359296 | tf_op jit(solution)/shard_map/all_gather | solution.py:215
  10.0 9.6 %collective-permute-start = (bf16[1,256,512]{2,1,0:T(8,128)(2,1)}, bf16[1,256,512]{2,1,0:T(8,128)(2,1)S(1)}, u32[]{:S(2)}, u32[]{:S(2)}) collective-permute-start(bf16[1,256,512]{2,1,0:T(8,128)(2,1)} %bitcast.64), channel_id=1, source_target_pairs={{0,4},{4,0},{8,12},{12,8},{16,20},{20,16},{24,28},{28,24},{1,5},{5... | collective-permute-start | bytes 786440 | tf_op jit(solution)/shard_map/ppermute | solution.py:24
  13.1 253.1 %reduce-scatter.2.cloned.1.call-start = ((), (), s32[]{:S(2)}) async-start(), calls=%async_computation.4 | async-start | bytes 2621440 | tf_op jit(solution)/shard_map/reduce_scatter | solution.py:218
  19.7 17.4 %collective-permute-start.1 = (bf16[2,256,512]{2,1,0:T(8,128)(2,1)S(1)}, bf16[2,256,512]{2,1,0:T(8,128)(2,1)S(1)}, u32[]{:S(2)}, u32[]{:S(2)}) collective-permute-start(bf16[2,256,512]{2,1,0:T(8,128)(2,1)S(1)} %get-tuple-element.12), channel_id=1, source_target_pairs={{0,8},{4,12},{8,0},{12,4},{16,24},{20,28},{24,16},{28,20},{1,9},{5... | collective-permute-start | bytes 1572872 | tf_op jit(solution)/shard_map/ppermute | solution.py:24
  37.4 61.8 %collective-permute-start.2 = (bf16[4,256,512]{2,1,0:T(8,128)(2,1)S(1)}, bf16[4,256,512]{2,1,0:T(8,128)(2,1)}, u32[]{:S(2)}, u32[]{:S(2)}) collective-permute-start(bf16[4,256,512]{2,1,0:T(8,128)(2,1)S(1)} %bitcast.52), channel_id=1, source_target_pairs={{0,16},{4,20},{8,24},{12,28},{16,0},{20,4},{24,8},{28,12},{1,17},{... | collective-permute-start | bytes 3145736 | tf_op jit(solution)/shard_map/ppermute | solution.py:24
  79.4 3.0 %copy-start.2 = (bf16[512,2048]{1,0:T(8,128)(2,1)S(1)}, bf16[512,2048]{1,0:T(8,128)(2,1)}, u32[]{:S(2)}) copy-start(bf16[512,2048]{1,0:T(8,128)(2,1)} %param.12) | copy-start | bytes 6291460
  100.7 1.8 copy-start.3
  180.7 3.0 %copy-start.5 = (f32[512,32]{0,1:T(8,128)S(1)}, f32[512,32]{0,1:T(8,128)}, u32[]{:S(2)}) copy-start(f32[512,32]{0,1:T(8,128)} %get-tuple-element.18) | copy-start | bytes 196612
  185.0 8.2 %copy-start.4 = (bf16[512,512]{0,1:T(8,128)(2,1)S(1)}, bf16[512,512]{0,1:T(8,128)(2,1)}, u32[]{:S(2)}) copy-start(bf16[512,512]{0,1:T(8,128)(2,1)} %fusion.11) | copy-start | bytes 1572868
Sparse Core Ops, SparseCore 0:
  9.5 67.5 all-gather.11
  79.2 51.5 all-gather.5
  132.9 47.7 all-gather.7
  182.6 49.5 all-gather.9
  236.5 29.5 reduce-scatter.1
